TPU v7x, 128 devices: a whole 4x4x4 slice. The times are simulated.
128 devices in a mesh: row: 8 (over y_lo, z), col: 2 (over y_hi), tensor: 8 (over x, core).
Axes of the slice: x: 4, y: 4 (y_hi: 2, y_lo: 2; y = y_hi * 2 + y_lo), z: 4, core: 2. Of those that a mesh axis runs over, the one named last changes fastest.
Arguments:
- tokens: bfloat16 [10240, 3072], P(('row', 'col', 'tensor')), may hold values from -6 to 6
- w_query: bfloat16 [3072, 3072], P(None, 'tensor'), may hold values from -0.109375 to 0.109375
- w_key: bfloat16 [3072, 3072], P(None, 'tensor'), may hold values from -0.109375 to 0.109375
- w_value: bfloat16 [3072, 3072], P(None, 'tensor'), may hold values from -0.109375 to 0.109375
- w_out: bfloat16 [3072, 3072], P('tensor'), may hold values from -0.109375 to 0.109375
- w_mod: bfloat16 [512, 18432], P(None, ('row', 'col', 'tensor')), may hold values from -2 to 2
- gain_query: float32 [64], replicated, may hold values from 0.5 to 2.5
- gain_key: float32 [64], replicated, may hold values from 0.5 to 2.5
- timesteps: int32 [2], replicated, may hold values from 0 to 999
- video_lengths: int32 [2], replicated, may hold values from 1 to 6117, 9788 in all
- piece_table: int32 [16], replicated, may hold values from 0 to 15, each once
Outputs:
- update: bfloat16 [10240, 3072], P(('row', 'col', 'tensor'))
Inputs may be any that keep to these rules, and one draw needn't show every extreme that they name: `video_lengths`: the two lengths sum to 9788; the larger one is at most 6117, and which sample has it varies. `piece_table`: each tile index 0 .. 15 appears once.
All inputs are finite; a program needn't handle non-finite values.
Results may differ from a plain program's by a relative error of at most 0.02.
Values may be sent and summed in bfloat16 or wider, within the bound.
No kernel may reach another device: no remote copies, remote signals or barrier semaphores. Data moves between devices by JAX's collectives and lax.ppermute only.
A program may use at most 192 MiB of HBM per device.

v0:
```python
import math
import jax
import jax.numpy as jnp
from jax import lax
from jax.sharding import PartitionSpec as P

HD = 64
TE = 512
TEXT = 226
HP = 30
WP = 45
CAP = 640


def slot_info(slot_ids, piece_table, video_lengths):
    tile_idx = slot_ids // CAP
    tile_total = piece_table.shape[0]
    placed = jnp.sum(
        jnp.where(
            tile_idx[:, None] == jnp.arange(tile_total, dtype=jnp.int32)[None, :],
            piece_table[None, :],
            0,
        ),
        axis=1,
    )
    token_id = placed * CAP + slot_ids % CAP
    boundary = TEXT + video_lengths[0]
    item_of = (token_id >= boundary).astype(jnp.int32)
    inner_idx = token_id - item_of * boundary
    is_text = inner_idx < TEXT
    video_idx = jnp.maximum(inner_idx - TEXT, 0)
    frame_idx = video_idx // (HP * WP)
    height_idx = video_idx // WP % HP
    width_idx = video_idx % WP
    return (item_of, is_text, frame_idx, height_idx, width_idx)


def time_features(timesteps):
    half_dim = TE // 2
    freqs = jnp.exp(-math.log(10000.0) * jnp.arange(half_dim, dtype=jnp.float32) / half_dim)
    angles = timesteps.astype(jnp.float32)[:, None] * freqs[None, :]
    return jnp.concatenate([jnp.cos(angles), jnp.sin(angles)], axis=1)


def rope_angles(frame_idx, height_idx, width_idx):
    time_dims = HD // 4
    space_dims = 3 * HD // 8
    freq_time = 10000.0 ** (-jnp.arange(0, time_dims, 2, dtype=jnp.float32) / time_dims)
    freq_space = 10000.0 ** (-jnp.arange(0, space_dims, 2, dtype=jnp.float32) / space_dims)
    return jnp.concatenate(
        [
            frame_idx.astype(jnp.float32)[:, None] * freq_time[None, :],
            height_idx.astype(jnp.float32)[:, None] * freq_space[None, :],
            width_idx.astype(jnp.float32)[:, None] * freq_space[None, :],
        ],
        axis=1,
    )


def head_prepare(projection, gain, angles, is_text):
    row_count = projection.shape[0]
    heads_here = projection.shape[1] // HD
    per_head = projection.reshape(row_count, heads_here, HD)
    center = per_head - jnp.mean(per_head, axis=2, keepdims=True)
    variance = jnp.mean(center * center, axis=2, keepdims=True)
    normed = center * lax.rsqrt(variance + 1e-06) * gain
    cosine = jnp.where(is_text[:, None], 1.0, jnp.cos(angles))[:, None, :]
    sine = jnp.where(is_text[:, None], 0.0, jnp.sin(angles))[:, None, :]
    paired = normed.reshape(row_count, heads_here, HD // 2, 2)
    even_part = paired[..., 0]
    odd_part = paired[..., 1]
    rotated = jnp.stack(
        [even_part * cosine - odd_part * sine, even_part * sine + odd_part * cosine], axis=-1
    )
    return rotated.reshape(row_count, heads_here * HD).astype(jnp.bfloat16)


def select_modulation(modulation, item_of, is_text, model_width):
    chosen = []
    for part_idx in range(3):
        video_cols = modulation[:, part_idx * model_width : (part_idx + 1) * model_width]
        text_cols = modulation[:, (part_idx + 3) * model_width : (part_idx + 4) * model_width]
        video_pick = jnp.where(
            item_of[:, None] == 1, video_cols[1][None, :], video_cols[0][None, :]
        )
        text_pick = jnp.where(item_of[:, None] == 1, text_cols[1][None, :], text_cols[0][None, :])
        chosen.append(jnp.where(is_text[:, None], text_pick, video_pick))
    return (chosen[0], chosen[1], chosen[2])


def modulate(tokens, shift, scale):
    values = tokens.astype(jnp.float32)
    center = values - jnp.mean(values, axis=1, keepdims=True)
    variance = jnp.mean(center * center, axis=1, keepdims=True)
    normed = center * lax.rsqrt(variance + 1e-05)
    return (normed * (1.0 + scale) + shift).astype(jnp.bfloat16)


def block_terms(query, key_part, value_part, same_item, heads_here):
    query_rows = query.shape[0]
    key_count = key_part.shape[0]
    query_heads = query.reshape(query_rows, heads_here, HD)
    key_heads = key_part.reshape(key_count, heads_here, HD)
    value_heads = value_part.reshape(key_count, heads_here, HD)
    scores = jnp.einsum(
        "qhd,khd->hqk", query_heads, key_heads, preferred_element_type=jnp.float32
    ) / math.sqrt(HD)
    weights = (jnp.exp(scores) * same_item[None, :, :]).astype(jnp.bfloat16)
    numer_add = jnp.einsum("hqk,khd->qhd", weights, value_heads, preferred_element_type=jnp.float32)
    denom_add = jnp.sum(weights.astype(jnp.float32), axis=2).T
    return (numer_add.reshape(query_rows, heads_here * HD), denom_add)


def local(
    tokens,
    w_query,
    w_key,
    w_value,
    w_out,
    w_mod,
    gain_query,
    gain_key,
    timesteps,
    video_lengths,
    piece_table,
):
    model_width = tokens.shape[1]
    act = jax.nn.silu(time_features(timesteps)).astype(jnp.bfloat16)
    partial_mod = jnp.dot(act, w_mod, preferred_element_type=jnp.float32)
    modulation = lax.all_gather(partial_mod, ("row", "col", "tensor"), axis=1, tiled=True)
    col_count = lax.axis_size("col")
    tile_here = lax.axis_index("row") * col_count + lax.axis_index("col")
    own_rows = tokens.shape[0]
    own_slots = (
        tile_here * CAP
        + lax.axis_index("tensor") * own_rows
        + jnp.arange(own_rows, dtype=jnp.int32)
    )
    own_item, own_text, own_frame, own_height, own_width = slot_info(
        own_slots, piece_table, video_lengths
    )
    shift, scale, gate = select_modulation(modulation, own_item, own_text, model_width)
    modded = modulate(tokens, shift, scale)
    pieces = lax.all_gather(modded, "tensor", axis=0, tiled=True)
    projected = jnp.concatenate(
        [
            jnp.dot(pieces, w_query, preferred_element_type=jnp.float32),
            jnp.dot(pieces, w_key, preferred_element_type=jnp.float32),
            jnp.dot(pieces, w_value, preferred_element_type=jnp.float32),
        ],
        axis=1,
    )
    local_width = w_query.shape[1]
    heads_here = local_width // HD
    tile_slots = tile_here * CAP + jnp.arange(CAP, dtype=jnp.int32)
    tile_item, tile_text, tile_frame, tile_height, tile_width = slot_info(
        tile_slots, piece_table, video_lengths
    )
    angles = rope_angles(tile_frame, tile_height, tile_width)
    query = head_prepare(projected[:, :local_width], gain_query, angles, tile_text)
    key_rows = head_prepare(
        projected[:, local_width : 2 * local_width], gain_key, angles, tile_text
    )
    value_rows = projected[:, 2 * local_width :].astype(jnp.bfloat16)
    key_block = lax.all_gather(key_rows, ("row", "col"), axis=0, tiled=True)
    value_block = lax.all_gather(value_rows, ("row", "col"), axis=0, tiled=True)
    numerator = jnp.zeros((CAP, local_width), jnp.float32)
    denominator = jnp.zeros((CAP, heads_here), jnp.float32)
    key_total = key_block.shape[0]
    key_slots = jnp.arange(key_total, dtype=jnp.int32)
    key_item, key_text, key_frame, key_height, key_width = slot_info(
        key_slots, piece_table, video_lengths
    )
    for offset in range(0, key_total, 512):
        stop = min(offset + 512, key_total)
        same_bool = tile_item[:, None] == key_item[None, offset:stop]
        same_item = same_bool.astype(jnp.float32)
        key_part = key_block[offset:stop]
        value_part = value_block[offset:stop]
        numer_add, denom_add = block_terms(query, key_part, value_part, same_item, heads_here)
        numerator = numerator + numer_add
        denominator = denominator + denom_add
    numerator, denominator = (numerator, denominator)
    attended = (numerator / jnp.repeat(denominator, HD, axis=1)).astype(jnp.bfloat16)
    projection = lax.psum_scatter(
        jnp.dot(attended, w_out, preferred_element_type=jnp.float32).astype(jnp.bfloat16),
        "tensor",
        scatter_dimension=0,
        tiled=True,
    ).astype(jnp.float32)
    return (gate * projection).astype(jnp.bfloat16)


def solution(mesh):
    placed = (
        P(("row", "col", "tensor"), None),
        P(None, "tensor"),
        P(None, "tensor"),
        P(None, "tensor"),
        P("tensor", None),
        P(None, ("row", "col", "tensor")),
        P(),
        P(),
        P(),
        P(),
        P(),
    )
    return jax.shard_map(
        local,
        mesh=mesh,
        in_specs=placed,
        out_specs=P(("row", "col", "tensor"), None),
        check_vma=False,
    )
```

profile of v0, /device:TPU:0, one launch (start us, length us, event | category | flops | bytes accessed | tf_op | source)
XLA Modules:
  0.0 762.9 jit_solution(14983908528028397755)
XLA Ops:
  12.6 179.5 %all-gather = f32[128,144,2]{1,2,0:T(2,128)S(1)} all-gather(f32[1,144,2]{1,2,0:T(2,128)S(1)} %convolution_bitcast_fusion.1), channel_id=1, replica_groups=mesh['row'=8,'col'=2,'tensor'=8] {'row','col','tensor'}, dimensions={0}, use_global_device_ids=true | all-gather | bytes 148608 | tf_op jit(solution)/shard_map/all_gather | solution.py:130
  195.5 24.6 %all-gather.5.cloned.1.call-done = bf16[640,3072]{1,0:T(8,128)(2,1)} async-done(((bf16[80,3072]{1,0:T(8,128)(2,1)}), bf16[640,3072]{1,0:T(8,128)(2,1)}) %all-gather.5.cloned.1.call-update) | async-done | bytes 3932176 | tf_op jit(solution)/shard_map/all_gather | solution.py:144
  220.2 5.8 convolution_convert_fusion.1
  228.5 4.9 fusion.47
  234.9 5.9 fusion.48
  249.0 3.3 subtract_convert_fusion
  256.6 8.8 %compare_convert_fusion.3 = (f32[640,512]{0,1:T(8,128)}, f32[640,512]{0,1:T(8,128)}, f32[640,512]{0,1:T(8,128)}, f32[640,512]{0,1:T(8,128)}, f32[640,512]{0,1:T(...) fusion(s32[640]{0:T(1024)S(1)} %get-tuple-element.105, ...), kind=kLoop, calls=%fused_computation.62 | loop fusion | flops 11796480 | bytes 23632384 | tf_op jit(solution)/shard_map/convert_element_type | solution.py:177
  267.5 161.6 %all-gather.7.cloned.1.call-done = bf16[10240,384]{1,0:T(8,128)(2,1)} async-done(((bf16[640,384]{1,0:T(8,128)(2,1)}), bf16[10240,384]{1,0:T(8,128)(2,1)}) %all-gather.7.cloned.1.call-update) | async-done | bytes 7864336 | tf_op jit(solution)/shard_map/all_gather | solution.py:166
  429.1 6.1 fusion.44
  469.6 152.2 %all-gather.9.cloned.1.call-done = bf16[10240,384]{0,1:T(8,128)(2,1)} async-done(((bf16[640,384]{0,1:T(8,128)(2,1)}), bf16[10240,384]{0,1:T(8,128)(2,1)}) %all-gather.9.cloned.1.call-update) | async-done | bytes 7864336 | tf_op jit(solution)/shard_map/all_gather | solution.py:165
  622.8 3.5 convert_reduce_fusion.19
  646.7 4.0 convert_reduce_fusion.12
  650.7 3.8 convert_reduce_fusion.11
  654.5 3.8 convert_reduce_fusion.10
  658.3 3.8 convert_reduce_fusion.9
  662.1 3.7 convert_reduce_fusion.8
  665.8 3.8 convert_reduce_fusion.7
  669.6 3.9 convert_reduce_fusion.6
  673.5 4.2 convert_reduce_fusion.5
  677.7 3.7 convert_reduce_fusion.4
  681.5 3.8 convert_reduce_fusion.2
  688.3 3.7 convert_reduce_fusion.1
  716.4 4.1 convolution_convert_fusion
  720.6 33.5 %reduce-scatter.2.cloned.1.call-done = bf16[80,3072]{1,0:T(8,128)(2,1)} async-done(((bf16[640,3072]{1,0:T(8,128)(2,1)}), bf16[80,3072]{1,0:T(8,128)(2,1)}) %reduce-scatter.2.cloned.1.call-update) | async-done | bytes 491536 | tf_op jit(solution)/shard_map/reduce_scatter | solution.py:185
  (252 shorter events, 111.8 us)
Async XLA Ops:
  6.5 709.9 %copy-start = (bf16[384,3072]{1,0:T(8,128)(2,1)S(1)}, bf16[384,3072]{1,0:T(8,128)(2,1)}, u32[]{:S(2)}) copy-start(bf16[384,3072]{1,0:T(8,128)(2,1)} %param.15) | copy-start | bytes 7077892
  6.5 213.6 %all-gather.5.cloned.1.call-start = ((), (), s32[]{:S(2)}) async-start(), calls=%async_computation.1 | async-start | bytes 4423680 | tf_op jit(solution)/shard_map/all_gather | solution.py:144
  11.4 214.6 %copy-start.62 = (pred[80]{0:T(512)(128)(4,1)}, pred[80]{0:T(512)(128)(4,1)S(1)}, u32[]{:S(2)}) copy-start(pred[80]{0:T(512)(128)(4,1)S(1)} %fusion.38) | copy-start | bytes 244
  195.4 30.9 %copy-start.66 = (f32[64]{0:T(128)S(1)}, f32[64]{0:T(128)}, u32[]{:S(2)}) copy-start(f32[64]{0:T(128)} %param.17) | copy-start | bytes 772
  195.4 31.6 %copy-start.67 = (f32[64]{0:T(128)S(1)}, f32[64]{0:T(128)}, u32[]{:S(2)}) copy-start(f32[64]{0:T(128)} %param.18) | copy-start | bytes 772
  195.5 32.4 %copy-start.64 = (s32[16]{0:T(128)S(1)}, s32[16]{0:T(128)}, u32[]{:S(2)}) copy-start(s32[16]{0:T(128)} %param.21) | copy-start | bytes 196
  195.5 233.7 %all-gather.7.cloned.1.call-start = ((), (), s32[]{:S(2)}) async-start(), calls=%async_computation.2 | async-start | bytes 8355840 | tf_op jit(solution)/shard_map/all_gather | solution.py:166
  226.0 395.8 %all-gather.9.cloned.1.call-start = ((), (), s32[]{:S(2)}) async-start(), calls=%async_computation.3 | async-start | bytes 8355840 | tf_op jit(solution)/shard_map/all_gather | solution.py:165
  249.0 5.5 copy-start.65
  254.4 499.6 %reduce-scatter.2.cloned.1.call-start = ((), (), s32[]{:S(2)}) async-start(), calls=%async_computation.4 | async-start | bytes 4423680 | tf_op jit(solution)/shard_map/reduce_scatter | solution.py:185
  256.6 8.8 %copy-start.10 = (bf16[640,6,32,1]{0,3,2,1:T(2,128)(2,1)S(1)}, bf16[640,6,32,1]{0,3,2,1:T(2,128)(2,1)}, u32[]{:S(2)}) copy-start(bf16[640,6,32,1]{0,3,2,1:T(2,128)(2,1)} %get-tuple-element.50) | copy-start | bytes 737284
  429.1 7.3 slice-start
  622.8 4.3 slice-start.1
  622.8 4.3 slice-start.2
  646.7 4.0 copy-start.38
  646.7 4.0 copy-start.55
  669.6 3.9 copy-start.32
  669.6 3.9 copy-start.49
  673.5 4.2 copy-start.31
  720.5 33.5 %copy-start.58 = (f32[1,3072]{1,0:T(1,128)S(1)}, f32[1,3072]{1,0:T(1,128)}, u32[]{:S(2)}) copy-start(f32[1,3072]{1,0:T(1,128)} %get-tuple-element.51) | copy-start | bytes 36868
  720.6 33.5 %copy-start.59 = (f32[1,3072]{1,0:T(1,128)S(1)}, f32[1,3072]{1,0:T(1,128)}, u32[]{:S(2)}) copy-start(f32[1,3072]{1,0:T(1,128)} %get-tuple-element.60) | copy-start | bytes 36868
  720.6 33.5 %copy-start.60 = (f32[1,3072]{1,0:T(1,128)S(1)}, f32[1,3072]{1,0:T(1,128)}, u32[]{:S(2)}) copy-start(f32[1,3072]{1,0:T(1,128)} %get-tuple-element.61) | copy-start | bytes 36868
  720.6 33.5 %copy-start.61 = (f32[1,3072]{1,0:T(1,128)S(1)}, f32[1,3072]{1,0:T(1,128)}, u32[]{:S(2)}) copy-start(f32[1,3072]{1,0:T(1,128)} %get-tuple-element.62) | copy-start | bytes 36868
  720.6 33.5 %copy-start.63 = (pred[80]{0:T(512)(128)(4,1)S(1)}, pred[80]{0:T(512)(128)(4,1)}, u32[]{:S(2)}) copy-start(pred[80]{0:T(512)(128)(4,1)} %copy-done.62) | copy-start | bytes 244
  (51 other events, 130.4 us)
Sparse Core Ops, SparseCore 0:
  195.6 24.5 all-gather.4
  226.1 202.9 all-gather.6
  430.8 190.9 all-gather.8
  720.7 33.2 reduce-scatter.1
where the time goes:
time: 768 us; the launch traced here: 763 us
  waiting for transfers between devices  372 us (48%)
  blocking collectives  180 us (23%)
  matrix products  104 us (14%)
  local copies, waits for them, and re-layouts  60.7 us (8%)
  other arithmetic  31.5 us (4%)
  between operations  15 us (2%)
    all_gather x1, blocking collectives, local(): lax.all_gather(partial_mod, ('row', 'col', 'tensor'), axis=1, tiled=True)  180 us
    all_gather x1, waiting for transfers between devices, local(): value_block = lax.all_gather(value_rows, ('row', 'col'), axis=0, tiled=True)  162 us
    all_gather x1, waiting for transfers between devices, local(): key_block = lax.all_gather(key_rows, ('row', 'col'), axis=0, tiled=True)  152 us
    dot_general x20, matrix products, block_terms(): jnp.einsum('qhd,khd->hqk', query_heads, key_heads, preferred_element_type...  61 us
    slice x23, local copies, waits for them, and re-layouts, local(): value_part = value_block[offset:stop]  40.4 us
    reduce_scatter x1, waiting for transfers between devices, local(): lax.psum_scatter(jnp.dot(attended, w_out, preferred_element_type=jnp.floa...  33.5 us
    all_gather x1, waiting for transfers between devices, local(): pieces = lax.all_gather(modded, 'tensor', axis=0, tiled=True)  24.6 us
    dot_general x20, matrix products, block_terms(): jnp.einsum('hqk,khd->qhd', weights, value_heads, preferred_element_type=j...  20.9 us
  transfers between devices with their start and end apart: 4, of which 4 were waited for; matrix products, arithmetic and copies ran while one was open for 11% of the time, Pallas kernels for 0%

commit v1 on v0

--- a/solution.py
+++ b/solution.py
@@ -141,7 +141,38 @@
     )
     shift, scale, gate = select_modulation(modulation, own_item, own_text, model_width)
     modded = modulate(tokens, shift, scale)
-    pieces = lax.all_gather(modded, "tensor", axis=0, tiled=True)
+    step_out, w2, o_now = (
+        jax.lax.psum(1, axis_name="tensor"),
+        jax.lax.axis_index("tensor"),
+        modded.shape[0],
+    )
+    shelf = []
+    for at, b in enumerate(modded.shape):
+        shelf.append(b * step_out if at == 0 else b)
+    pieces = lax.dynamic_update_slice_in_dim(
+        jnp.zeros(shelf, modded.dtype), modded, w2 * o_now, axis=0
+    )
+    u1 = odd = modded
+    kk = 1
+    while kk < step_out // 2 + 1:
+        steps_seen = []
+        at = 0
+        while at < step_out:
+            steps_seen.append((at, (at + 1) % step_out))
+            at += 1
+        u1 = jax.lax.ppermute(u1, axis_name="tensor", perm=steps_seen)
+        pieces = lax.dynamic_update_slice_in_dim(pieces, u1, (w2 - kk) % step_out * o_now, axis=0)
+        if 2 * kk < step_out:
+            runs = []
+            at = 0
+            while at < step_out:
+                runs.append((at, (at - 1) % step_out))
+                at = at + 1
+            odd = jax.lax.ppermute(odd, axis_name="tensor", perm=runs)
+            pieces = lax.dynamic_update_slice_in_dim(
+                pieces, odd, (w2 + kk) % step_out * o_now, axis=0
+            )
+        kk += 1
     projected = jnp.concatenate(
         [
             jnp.dot(pieces, w_query, preferred_element_type=jnp.float32),

time: 768 us -> 799 us (1.040)
  matrix products: 104 us -> 123 us
  local copies, waits for them, and re-layouts: 60.7 us -> 70.7 us
  starting transfers between devices: 0.42 us -> 9.25 us
    all_gather x1 -> x0, waiting for transfers between devices: 24.6 us -> none  [local(): pieces = lax.all_gather(modded, 'tensor', axis=0, tiled=True)]
    ppermute x0 -> x7, waiting for transfers between devices: none -> 24.3 us  [the longest x4 24.3 us: local(): u1 = jax.lax.ppermute(u1, axis_name='tensor', perm=steps_seen)]
    dot_general x20, matrix products: 61 us -> 81.5 us  [block_terms(): jnp.einsum('qhd,khd->hqk', query_heads, key_heads, preferred_element_type...]
    ppermute x0 -> x7, starting transfers between devices: none -> 8.87 us  [the longest x3 8.53 us: local(): odd = jax.lax.ppermute(odd, axis_name='tensor', perm=runs)]
  transfers between devices with their start and end apart: 4 -> 10, of which waited for: 4 -> 7; matrix products, arithmetic and copies ran while one was open for 11% -> 11% of each run, Pallas kernels for 0% -> 0%
where the time goes in v1:
time: 799 us; the launch traced here: 793 us
  waiting for transfers between devices  365 us (46%)
  blocking collectives  180 us (23%)
  matrix products  123 us (15%)
  local copies, waits for them, and re-layouts  70.7 us (9%)
  other arithmetic  30.6 us (4%)
  between operations  15 us (2%)
  starting transfers between devices  9.25 us (1%)
    all_gather x1, blocking collectives, local(): lax.all_gather(partial_mod, ('row', 'col', 'tensor'), axis=1, tiled=True)  180 us
    all_gather x1, waiting for transfers between devices, local(): value_block = lax.all_gather(value_rows, ('row', 'col'), axis=0, tiled=True)  155 us
    all_gather x1, waiting for transfers between devices, local(): key_block = lax.all_gather(key_rows, ('row', 'col'), axis=0, tiled=True)  152 us
    dot_general x20, matrix products, block_terms(): jnp.einsum('qhd,khd->hqk', query_heads, key_heads, preferred_element_type...  81.5 us
    slice x23, local copies, waits for them, and re-layouts, local(): value_part = value_block[offset:stop]  40.4 us
    reduce_scatter x1, waiting for transfers between devices, local(): lax.psum_scatter(jnp.dot(attended, w_out, preferred_element_type=jnp.floa...  33.5 us
    ppermute x4, waiting for transfers between devices, local(): u1 = jax.lax.ppermute(u1, axis_name='tensor', perm=steps_seen)  24.3 us
    dot_general x20, matrix products, block_terms(): jnp.einsum('hqk,khd->qhd', weights, value_heads, preferred_element_type=j...  20.8 us
  transfers between devices with their start and end apart: 10, of which 7 were waited for; matrix products, arithmetic and copies ran while one was open for 11% of the time, Pallas kernels for 0%

profile of v1, /device:TPU:0, one launch (start us, length us, event | category | flops | bytes accessed | tf_op | source)
XLA Modules:
  0.0 793.3 jit_solution(7071441534848822220)
XLA Ops:
  12.6 179.5 %all-gather = f32[128,144,2]{1,2,0:T(2,128)S(1)} all-gather(f32[1,144,2]{1,2,0:T(2,128)S(1)} %convolution_bitcast_fusion.1), channel_id=1, replica_groups=mesh['row'=8,'col'=2,'tensor'=8] {'row','col','tensor'}, dimensions={0}, use_global_device_ids=true | all-gather | bytes 148608 | tf_op jit(solution)/shard_map/all_gather | solution.py:130
  199.8 6.7 collective-permute-done
  211.1 4.9 collective-permute-done.2
  220.6 4.9 collective-permute-done.4
  227.0 7.8 collective-permute-done.6
  235.7 5.1 convolution_convert_fusion.1
  243.3 4.9 fusion.48
  249.8 5.9 fusion.49
  271.5 9.0 %compare_convert_fusion.3 = (f32[640,512]{0,1:T(8,128)}, f32[640,512]{0,1:T(8,128)}, f32[640,512]{0,1:T(8,128)}, f32[640,512]{0,1:T(8,128)}, f32[640,512]{0,1:T(...) fusion(s32[640]{0:T(1024)S(1)} %get-tuple-element.107, ...), kind=kLoop, calls=%fused_computation.62 | loop fusion | flops 11796480 | bytes 23632384 | tf_op jit(solution)/shard_map/convert_element_type | solution.py:208
  282.5 154.9 %all-gather.4.cloned.1.call-done = bf16[10240,384]{1,0:T(8,128)(2,1)} async-done(((bf16[640,384]{1,0:T(8,128)(2,1)}), bf16[10240,384]{1,0:T(8,128)(2,1)}) %all-gather.4.cloned.1.call-update) | async-done | bytes 7864336 | tf_op jit(solution)/shard_map/all_gather | solution.py:197
  437.4 6.1 fusion.45
  477.9 152.2 %all-gather.6.cloned.1.call-done = bf16[10240,384]{0,1:T(8,128)(2,1)} async-done(((bf16[640,384]{0,1:T(8,128)(2,1)}), bf16[10240,384]{0,1:T(8,128)(2,1)}) %all-gather.6.cloned.1.call-update) | async-done | bytes 7864336 | tf_op jit(solution)/shard_map/all_gather | solution.py:196
  630.1 5.5 fusion.44
  662.1 5.7 convert_reduce_fusion.11
  667.8 5.7 convert_reduce_fusion.10
  673.5 5.7 convert_reduce_fusion.9
  679.2 5.7 convert_reduce_fusion.8
  684.9 5.7 convert_reduce_fusion.7
  690.6 5.7 convert_reduce_fusion.6
  696.3 6.2 convert_reduce_fusion.5
  702.5 5.8 convert_reduce_fusion.4
  708.3 5.7 convert_reduce_fusion.2
  716.9 6.0 convert_reduce_fusion.1
  751.0 33.5 %reduce-scatter.2.cloned.1.call-done = bf16[80,3072]{1,0:T(8,128)(2,1)} async-done(((bf16[640,3072]{1,0:T(8,128)(2,1)}), bf16[80,3072]{1,0:T(8,128)(2,1)}) %reduce-scatter.2.cloned.1.call-update) | async-done | bytes 491536 | tf_op jit(solution)/shard_map/reduce_scatter | solution.py:216
  (285 shorter events, 139.8 us)
Async XLA Ops:
  6.5 740.3 %copy-start = (bf16[384,3072]{1,0:T(8,128)(2,1)S(1)}, bf16[384,3072]{1,0:T(8,128)(2,1)}, u32[]{:S(2)}) copy-start(bf16[384,3072]{1,0:T(8,128)(2,1)} %param.15) | copy-start | bytes 7077892
  6.5 187.1 %copy-start.1 = (bf16[80,3072]{1,0:T(8,128)(2,1)S(1)}, bf16[80,3072]{1,0:T(8,128)(2,1)}, u32[]{:S(2)}) copy-start(bf16[80,3072]{1,0:T(8,128)(2,1)} %param.11) | copy-start | bytes 1474564
  6.5 430.9 %all-gather.4.cloned.1.call-start = ((), (), s32[]{:S(2)}) async-start(), calls=%async_computation.1 | async-start | bytes 8355840 | tf_op jit(solution)/shard_map/all_gather | solution.py:197
  11.4 183.5 %copy-start.70 = (pred[80]{0:T(512)(128)(4,1)}, pred[80]{0:T(512)(128)(4,1)S(1)}, u32[]{:S(2)}) copy-start(pred[80]{0:T(512)(128)(4,1)S(1)} %fusion.38) | copy-start | bytes 244
  196.8 9.7 %collective-permute-start = (bf16[80,3072]{1,0:T(8,128)(2,1)}, bf16[80,3072]{1,0:T(8,128)(2,1)S(1)}, u32[]{:S(2)}, u32[]{:S(2)}) collective-permute-start(bf16[80,3072]{1,0:T(8,128)(2,1)} %get-tuple-element.6), channel_id=1, source_target_pairs={{0,1},{1,2},{2,3},{3,4},{4,5},{5,6},{6,7},{7,0},{8,9},{9,10},{10,1... | collective-permute-start | bytes 1474568 | tf_op jit(solution)/shard_map/ppermute | solution.py:163
  197.2 9.3 %collective-permute-start.1 = (bf16[80,3072]{1,0:T(8,128)(2,1)}, bf16[80,3072]{1,0:T(8,128)(2,1)S(1)}, u32[]{:S(2)}, u32[]{:S(2)}) collective-permute-start(bf16[80,3072]{1,0:T(8,128)(2,1)} %get-tuple-element.6), channel_id=1, source_target_pairs={{0,7},{1,0},{2,1},{3,2},{4,3},{5,4},{6,5},{7,6},{8,15},{9,8},{10,9... | collective-permute-start | bytes 1474568 | tf_op jit(solution)/shard_map/ppermute | solution.py:171
  199.8 36.0 %copy-start.76 = (bf16[3072,384]{1,0:T(8,128)(2,1)S(1)}, bf16[3072,384]{1,0:T(8,128)(2,1)}, u32[]{:S(2)}) copy-start(bf16[3072,384]{1,0:T(8,128)(2,1)} %param.14) | copy-start | bytes 7077892
  206.5 9.5 %collective-permute-start.2 = (bf16[80,3072]{1,0:T(8,128)(2,1)S(1)}, bf16[80,3072]{1,0:T(8,128)(2,1)S(1)}, u32[]{:S(2)}, u32[]{:S(2)}) collective-permute-start(bf16[80,3072]{1,0:T(8,128)(2,1)S(1)} %collective-permute-done), channel_id=1, source_target_pairs={{0,1},{1,2},{2,3},{3,4},{4,5},{5,6},{6,7},{7,0},{8,9},{9,10},{10,1... | collective-permute-start | bytes 1474568 | tf_op jit(solution)/shard_map/ppermute | solution.py:163
  206.5 9.5 %collective-permute-start.3 = (bf16[80,3072]{1,0:T(8,128)(2,1)S(1)}, bf16[80,3072]{1,0:T(8,128)(2,1)S(1)}, u32[]{:S(2)}, u32[]{:S(2)}) collective-permute-start(bf16[80,3072]{1,0:T(8,128)(2,1)S(1)} %collective-permute-done.1), channel_id=1, source_target_pairs={{0,7},{1,0},{2,1},{3,2},{4,3},{5,4},{6,5},{7,6},{8,15},{9,8},{10,9... | collective-permute-start | bytes 1474568 | tf_op jit(solution)/shard_map/ppermute | solution.py:171
  216.0 9.5 %collective-permute-start.4 = (bf16[80,3072]{1,0:T(8,128)(2,1)S(1)}, bf16[80,3072]{1,0:T(8,128)(2,1)S(1)}, u32[]{:S(2)}, u32[]{:S(2)}) collective-permute-start(bf16[80,3072]{1,0:T(8,128)(2,1)S(1)} %collective-permute-done.2), channel_id=1, source_target_pairs={{0,1},{1,2},{2,3},{3,4},{4,5},{5,6},{6,7},{7,0},{8,9},{9,10},{10,1... | collective-permute-start | bytes 1474568 | tf_op jit(solution)/shard_map/ppermute | solution.py:163
  216.0 10.3 %collective-permute-start.5 = (bf16[80,3072]{1,0:T(8,128)(2,1)S(1)}, bf16[80,3072]{1,0:T(8,128)(2,1)S(1)}, u32[]{:S(2)}, u32[]{:S(2)}) collective-permute-start(bf16[80,3072]{1,0:T(8,128)(2,1)S(1)} %collective-permute-done.3), channel_id=1, source_target_pairs={{0,7},{1,0},{2,1},{3,2},{4,3},{5,4},{6,5},{7,6},{8,15},{9,8},{10,9... | collective-permute-start | bytes 1474568 | tf_op jit(solution)/shard_map/ppermute | solution.py:171
  225.4 9.5 %collective-permute-start.6 = (bf16[80,3072]{1,0:T(8,128)(2,1)S(1)}, bf16[80,3072]{1,0:T(8,128)(2,1)S(1)}, u32[]{:S(2)}, u32[]{:S(2)}) collective-permute-start(bf16[80,3072]{1,0:T(8,128)(2,1)S(1)} %collective-permute-done.4), channel_id=1, source_target_pairs={{0,1},{1,2},{2,3},{3,4},{4,5},{5,6},{6,7},{7,0},{8,9},{9,10},{10,1... | collective-permute-start | bytes 1474568 | tf_op jit(solution)/shard_map/ppermute | solution.py:163
  235.7 6.2 copy-start.75
  235.7 7.0 copy-start.72
  240.9 389.2 %all-gather.6.cloned.1.call-start = ((), (), s32[]{:S(2)}) async-start(), calls=%async_computation.2 | async-start | bytes 8355840 | tf_op jit(solution)/shard_map/all_gather | solution.py:196
  269.4 515.1 %reduce-scatter.2.cloned.1.call-start = ((), (), s32[]{:S(2)}) async-start(), calls=%async_computation.3 | async-start | bytes 4423680 | tf_op jit(solution)/shard_map/reduce_scatter | solution.py:216
  271.5 9.0 %copy-start.11 = (bf16[640,6,32,1]{0,3,2,1:T(2,128)(2,1)S(1)}, bf16[640,6,32,1]{0,3,2,1:T(2,128)(2,1)}, u32[]{:S(2)}) copy-start(bf16[640,6,32,1]{0,3,2,1:T(2,128)(2,1)} %get-tuple-element.52) | copy-start | bytes 737284
  437.4 7.3 slice-start
  696.3 6.2 copy-start.41
  751.0 33.5 %copy-start.51 = (f32[1,3072]{1,0:T(1,128)S(1)}, f32[1,3072]{1,0:T(1,128)}, u32[]{:S(2)}) copy-start(f32[1,3072]{1,0:T(1,128)} %get-tuple-element.53) | copy-start | bytes 36868
  751.0 33.5 %copy-start.52 = (f32[1,3072]{1,0:T(1,128)S(1)}, f32[1,3072]{1,0:T(1,128)}, u32[]{:S(2)}) copy-start(f32[1,3072]{1,0:T(1,128)} %get-tuple-element.62) | copy-start | bytes 36868
  751.0 33.5 %copy-start.53 = (f32[1,3072]{1,0:T(1,128)S(1)}, f32[1,3072]{1,0:T(1,128)}, u32[]{:S(2)}) copy-start(f32[1,3072]{1,0:T(1,128)} %get-tuple-element.63) | copy-start | bytes 36868
  751.0 33.5 %copy-start.54 = (f32[1,3072]{1,0:T(1,128)S(1)}, f32[1,3072]{1,0:T(1,128)}, u32[]{:S(2)}) copy-start(f32[1,3072]{1,0:T(1,128)} %get-tuple-element.64) | copy-start | bytes 36868
  751.0 33.5 %copy-start.71 = (pred[80]{0:T(512)(128)(4,1)S(1)}, pred[80]{0:T(512)(128)(4,1)}, u32[]{:S(2)}) copy-start(pred[80]{0:T(512)(128)(4,1)} %copy-done.70) | copy-start | bytes 244
  (65 other events, 165.2 us)
Sparse Core Ops, SparseCore 0:
  241.0 196.3 all-gather.3
  439.1 190.9 all-gather.5
  751.2 33.2 reduce-scatter.1
